TPU v7x, 32 devices: a whole 2x2x4 slice. The times are simulated.
32 devices in a mesh: dp: 8 (over z, x), rep: 4 (over y, core).
Axes of the slice: x: 2, y: 2, z: 4, core: 2. Of those that a mesh axis runs over, the one named last changes fastest.
Arguments:
- hot_ids: int32 [8192, 2], P(('dp', 'rep')), may hold values from 0 to 1023
- cold_owner: int32 [16384, 1], P(('dp', 'rep')), may hold values from 0 to 7; in each aligned block of 512 rows (0 to 511, 512 to 1023, ...) at most 128 rows name the same one
- cold_offset: int32 [16384], P(('dp', 'rep')), may hold values from 0 to 511
- labels: int32 [8192], P(('dp', 'rep')), may hold values 0 or 1
- top_weight: bfloat16 [512, 1024], replicated, may hold values from -0.25 to 0.25
- out_weight: float32 [1024], replicated, may hold values from -0.5 to 0.5
- cold_table: float32 [4096, 128], P('dp'), may hold values from -6 to 6
- cold_accum: float32 [4096, 128], P('dp'), may hold values from 0.0001 to 0.01
- hot_cache: float32 [1024, 128], replicated, may hold values from -6 to 6
- hot_accum: float32 [1024, 128], replicated, may hold values from 0.01 to 1
- pending: float32 [32768, 128], P(('dp', 'rep')), may hold values from -0.3 to 0.3
- refresh_blocks: int32 [3], replicated, may hold values from 0 to 7, as said below
- block_clock: int32 [8], replicated, may hold values from 0 to 8
Outputs:
- cold_table_new: float32 [4096, 128], P('dp')
- cold_accum_new: float32 [4096, 128], P('dp')
- hot_cache_new: float32 [1024, 128], replicated
- hot_accum_new: float32 [1024, 128], replicated
- pending_new: float32 [32768, 128], P(('dp', 'rep'))
- top_grad: float32 [512, 1024], P(('dp', 'rep'))
- out_grad: float32 [1024], replicated
Inputs may be any that keep to these rules, and one draw needn't show every extreme that they name: `cold_owner`: within the lookups of one device (512 rows), no owner is named more than 128 times. `refresh_blocks`: the block numbers are distinct.
All inputs are finite; a program needn't handle non-finite values. No bound on the sum of `labels` on one device may be relied on, other than what follows from the above.
Results may differ from a plain program's by a relative error of at most 0.00165.
The roundings to bfloat16 on the way count: a program that leaves them out, or rounds other values in their place, can miss the bound.
Values may be sent and summed in bfloat16 or wider, within the bound.
A program may use at most 64 MiB of HBM per device.

v0:
```python
import jax
import jax.numpy as jnp
from jax import lax
from jax.sharding import PartitionSpec as P

BLOCK = 128
step_size = 0.5
epsilon = 1e-08


def adagrad(table_rows, accum_rows, gradient):
    accum_next = accum_rows + gradient * gradient
    return (table_rows - step_size * gradient / (jnp.sqrt(accum_next) + epsilon), accum_next)


def local(
    hot_ids,
    cold_owner,
    cold_offset,
    labels,
    top_weight,
    out_weight,
    cold_table,
    cold_accum,
    hot_cache,
    hot_accum,
    pending,
    refresh_blocks,
    block_clock,
):
    width = hot_cache.shape[1]
    samples = hot_ids.shape[0]
    hot_feats = hot_ids.shape[1]
    lookups = cold_offset.shape[0]
    cold_feats = lookups // samples
    owners_count = lax.axis_size("dp")
    capacity = max(2, 2 * lookups // owners_count)
    owners = cold_owner[:, 0]
    matches = (owners[:, None] == jnp.arange(owners_count, dtype=jnp.int32)[None, :]).astype(
        jnp.int32
    )
    earlier = jnp.cumsum(matches, axis=0) - matches
    positions = jnp.sum(earlier * matches, axis=1)
    targets = owners * capacity + positions
    requests = jnp.zeros((owners_count * capacity,), jnp.int32).at[targets].set(cold_offset)
    requests = requests.reshape(owners_count, capacity)
    asked = lax.all_to_all(requests, "dp", split_axis=0, concat_axis=0, tiled=True)
    found = cold_table[asked].astype(jnp.bfloat16)
    returned = lax.all_to_all(found, "dp", split_axis=0, concat_axis=0, tiled=True)
    cold_rows = returned.reshape(owners_count * capacity, width)[targets]
    cold_rows = cold_rows.reshape(samples, cold_feats, width)
    hot_rows = hot_cache[hot_ids].astype(jnp.bfloat16)
    inputs = jnp.concatenate([hot_rows, cold_rows], axis=1).reshape(
        samples, (hot_feats + cold_feats) * width
    )
    preact = jnp.dot(inputs, top_weight, preferred_element_type=jnp.float32)
    hidden = jax.nn.silu(preact).astype(jnp.bfloat16)
    hidden_wide = hidden.astype(jnp.float32)
    logits = jnp.dot(hidden_wide, out_weight, precision=lax.Precision.HIGHEST)
    errors = jax.nn.sigmoid(logits) - labels.astype(jnp.float32)
    gates = jax.nn.sigmoid(preact)
    slope = gates * (1.0 + preact * (1.0 - gates))
    dhidden = (errors[:, None] * out_weight[None, :] * slope).astype(jnp.bfloat16)
    head_term = jnp.dot(errors, hidden_wide, precision=lax.Precision.HIGHEST)
    top_grad = lax.psum_scatter(
        lax.dot_general(
            inputs, dhidden, (((0,), (0,)), ((), ())), preferred_element_type=jnp.float32
        ),
        ("dp", "rep"),
        scatter_dimension=0,
        tiled=True,
    )
    dinputs = lax.dot_general(
        dhidden, top_weight, (((1,), (1,)), ((), ())), preferred_element_type=jnp.float32
    ).astype(jnp.bfloat16)
    dinputs = dinputs.reshape(samples, hot_feats + cold_feats, width)
    cold_dx = dinputs[:, hot_feats:].reshape(lookups, width)
    outgoing = jnp.zeros((owners_count * capacity, width), jnp.bfloat16).at[targets].set(cold_dx)
    outgoing = outgoing.reshape(owners_count, capacity, width)
    incoming = lax.all_to_all(outgoing, "dp", split_axis=0, concat_axis=0, tiled=True)
    own_rows = cold_table.shape[0]
    cold_grad = (
        jnp.zeros((own_rows, width), jnp.float32)
        .at[asked.reshape(-1)]
        .add(incoming.reshape(-1, width).astype(jnp.float32))
    )
    quarter = own_rows // lax.axis_size("rep")
    offset_rows = lax.axis_index("rep") * quarter
    cold_share = lax.psum_scatter(cold_grad, "rep", scatter_dimension=0, tiled=True)
    table_share = lax.dynamic_slice_in_dim(cold_table, offset_rows, quarter, 0)
    accum_share = lax.dynamic_slice_in_dim(cold_accum, offset_rows, quarter, 0)
    table_updated, accum_updated = adagrad(table_share, accum_share, cold_share)
    cold_table_new, cold_accum_new = (
        lax.all_gather(table_updated, "rep", axis=0, tiled=True),
        lax.all_gather(accum_updated, "rep", axis=0, tiled=True),
    )
    hot_count = hot_cache.shape[0]
    blocks_count = hot_count // BLOCK
    hot_dx = dinputs[:, :hot_feats].reshape(samples * hot_feats, width).astype(jnp.float32)
    hot_grad = jnp.zeros((hot_count, width), jnp.float32).at[hot_ids.reshape(-1)].add(hot_dx)
    carried = (pending + hot_grad).reshape(blocks_count, BLOCK, width)
    picked = carried[refresh_blocks]
    divisors = 1.0 + block_clock[refresh_blocks].astype(jnp.float32)
    cache_blocks = hot_cache.reshape(blocks_count, BLOCK, width)
    accum_blocks = hot_accum.reshape(blocks_count, BLOCK, width)
    cache_chosen = cache_blocks[refresh_blocks]
    accum_chosen = accum_blocks[refresh_blocks]
    picked_sum, out_grad = lax.psum((picked, head_term), ("dp", "rep"))
    flush = picked_sum / divisors[:, None, None]
    cache_part, accum_part = adagrad(cache_chosen, accum_chosen, flush)
    hot_cache_new = cache_blocks.at[refresh_blocks].set(cache_part).reshape(hot_count, width)
    hot_accum_new = accum_blocks.at[refresh_blocks].set(accum_part).reshape(hot_count, width)
    pending_new = carried.at[refresh_blocks].set(0.0).reshape(hot_count, width)
    return (
        cold_table_new,
        cold_accum_new,
        hot_cache_new,
        hot_accum_new,
        pending_new,
        top_grad,
        out_grad,
    )


def solution(mesh):
    in_specs = (
        P(("dp", "rep"), None),
        P(("dp", "rep"), None),
        P(("dp", "rep")),
        P(("dp", "rep")),
        P(),
        P(),
        P("dp", None),
        P("dp", None),
        P(),
        P(),
        P(("dp", "rep"), None),
        P(),
        P(),
    )
    out_specs = (
        P("dp", None),
        P("dp", None),
        P(),
        P(),
        P(("dp", "rep"), None),
        P(("dp", "rep"), None),
        P(),
    )
    return jax.shard_map(local, mesh=mesh, in_specs=in_specs, out_specs=out_specs, check_vma=False)
```

profile of v0, /device:TPU:0, one launch (start us, length us, event | category | flops | bytes accessed | tf_op | source)
XLA Modules:
  0.0 244.3 jit_solution(7436814418134962637)
XLA Ops:
  8.0 1.2 copy.44
  9.4 1.1 reduce-window.6
  10.9 2.6 %scatter_custom_fusion = s32[1024]{0:T(1024)S(1)} fusion(s32[512]{0:T(512)S(1)} %bitcast.83, s32[512]{0:T(512)} %param.15, s32[]{:T(128)} %constant.13.clone.1), kind=kCustom, calls=%fused_computation.55 | custom fusion | bytes 4608 | tf_op jit(solution)/shard_map/scatter | solution.py:45
  13.5 13.6 %all_to_all.22 = s32[8,1,128]{2,1,0:T(1,128)S(1)} all-to-all(s32[8,1,128]{2,1,0:T(1,128)S(1)} %bitcast.82), channel_id=1, replica_groups=mesh['dp'=8,'rep'=4] {'dp'}, dimensions={0} | all-to-all | bytes 8192 | tf_op jit(solution)/shard_map/all_to_all | solution.py:47
  27.1 4.1 %gather_fusion.1 = bf16[1024,128]{1,0:T(8,128)(2,1)} fusion(f32[512,128]{1,0:T(8,128)S(1)} %copy-done.2, s32[1024]{0:T(1024)S(1)} %fusion.17), kind=kCustom, calls=%fused_computation.1 | custom fusion | bytes 528384 | tf_op jit(solution)/shard_map/gather | solution.py:48
  31.2 3.4 %all-to-all-start.1 = ((bf16[8,128,128]{2,1,0:T(8,128)(2,1)}), bf16[8,128,128]{2,1,0:T(8,128)(2,1)S(1)}, u32[]{:S(2)}, u32[]{:S(2)}) async-start(bf16[8,128,128]{2,1,0:T(8,128)(2,1)} %bitcast.12), calls=%async_computation.1 | async-start | bytes 524288 | tf_op jit(solution)/shard_map/all_to_all | solution.py:49
  35.0 1.1 gather_fusion
  36.6 6.2 %all-to-all-done.1 = bf16[8,128,128]{2,1,0:T(8,128)(2,1)S(1)} async-done(((bf16[8,128,128]{2,1,0:T(8,128)(2,1)}), bf16[8,128,128]{2,1,0:T(8,128)(2,1)S(1)}, u32[]{:S(2)}, u32[]{:S(2)}) %all-to-all-start.1) | async-done | bytes 262176 | tf_op jit(solution)/shard_map/all_to_all | solution.py:49
  42.8 1.3 gather_fusion.2
  46.3 1.3 convolution_convert_fusion
  47.6 1.8 reshape.179
  49.4 1.9 fusion.20
  51.3 2.8 %scatter_custom_fusion.1 = bf16[1024,128]{1,0:T(8,128)(2,1)} fusion(s32[512]{0:T(512)S(1)} %bitcast.85, bf16[512,128]{1,0:T(8,128)(2,1)} %bitcast.77, bf16[]{:T(256)} %constant.17.clone.1), kind=kCustom, calls=%fused_computation.31 | custom fusion | bytes 262656 | tf_op jit(solution)/shard_map/scatter | solution.py:78
  54.1 4.0 %all-to-all-start.2 = ((bf16[8,128,128]{2,1,0:T(8,128)(2,1)}), bf16[8,128,128]{2,1,0:T(8,128)(2,1)}, u32[]{:S(2)}, u32[]{:S(2)}) async-start(bf16[8,128,128]{2,1,0:T(8,128)(2,1)} %bitcast.71), calls=%async_computation.2 | async-start | bytes 524288 | tf_op jit(solution)/shard_map/all_to_all | solution.py:80
  58.2 0.8 copy.22
  59.0 1.1 reshape.183
  60.6 3.6 %scatter_custom_fusion.3 = f32[1024,128]{1,0:T(8,128)S(1)} fusion(f32[1024,128]{1,0:T(8,128)S(1)} %copy-done.6, s32[512]{0:T(512)} %bitcast.91, bf16[512,128]{1,0:T(8,128)(2,1)S(1)} %bitcast.72), kind=kCustom, calls=%fused_computation.25 | custom fusion | flops 131072 | bytes 655360 | tf_op jit(solution)/shard_map/scatter-add | solution.py:100
  64.3 1.2 gather_fusion.4
  65.6 0.7 all-to-all-done.2
  66.3 7.1 %scatter_custom_fusion.2 = f32[512,128]{1,0:T(8,128)} fusion(s32[1024]{0:T(1024)S(1)} %bitcast.90, bf16[1024,128]{1,0:T(8,128)(2,1)} %bitcast.31, f32[]{:T(128)} %constant.15.clone.1), kind=kCustom, calls=%fused_computation.18 | custom fusion | flops 262144 | bytes 524292 | tf_op jit(solution)/shard_map/scatter-add | solution.py:85
  73.7 3.4 %fusion.2 = f32[512,1024]{1,0:T(8,128)} fusion(bf16[32,8,4,128]{3,2,1,0:T(4,128)(2,1)} %bitcast.76, f32[256,1024]{1,0:T(8,128)} %copy-done.18, f32[1024]{0:T(1024)} %param.18, f32[256]{0:T(256)S(1)} %copy-done.15), kind=kOutput, calls=%fused_computation.20 | convolution fusion | flops 271056896 | bytes 3412992 | tf_op jit(solution)/shard_map/dot_general | solution.py:66
  78.3 1.2 gather_fusion.3
  79.6 1.2 gather_fusion.6
  81.5 1.5 scatter_fusion.2
  83.4 41.0 %psum.15 = f32[1024]{0:T(1024)} all-reduce(f32[1024]{0:T(1024)S(1)} %bitcast.81), channel_id=1, replica_groups=mesh['dp'=8,'rep'=4] {'dp','rep'}, use_global_device_ids=true, to_apply=%region_13.14 | all-reduce | flops 1024 | bytes 8192 | tf_op jit(solution)/shard_map/psum | solution.py:108
  124.4 67.7 %all-reduce.2.cloned.1.call-done = f32[3,128,128]{2,1,0:T(8,128)} async-done(((f32[3,128,128]{2,1,0:T(8,128)}), f32[3,128,128]{2,1,0:T(8,128)}) %all-reduce.2.cloned.1.call-update) | async-done | bytes 196624 | tf_op jit(solution)/shard_map/psum | solution.py:108
  192.1 1.3 multiply_add_fusion
  194.8 1.1 multiply_add_fusion.1
  195.8 6.4 %all_gather.7 = f32[512,128]{1,0:T(8,128)S(1)} all-gather(f32[128,128]{1,0:T(8,128)S(1)} %get-tuple-element.9), channel_id=1, replica_groups=mesh['dp'=8,'rep'=4] {'rep'}, dimensions={0}, use_global_device_ids=true | all-gather | bytes 327680 | tf_op jit(solution)/shard_map/all_gather | solution.py:95
  202.2 6.1 %all_gather.6 = f32[512,128]{1,0:T(8,128)S(1)} all-gather(f32[128,128]{1,0:T(8,128)S(1)} %get-tuple-element.10), channel_id=1, replica_groups=mesh['dp'=8,'rep'=4] {'rep'}, dimensions={0}, use_global_device_ids=true | all-gather | bytes 327680 | tf_op jit(solution)/shard_map/all_gather | solution.py:94
  208.3 27.2 %reduce-scatter.5.cloned.1.call-done = f32[16,1024]{1,0:T(8,128)} async-done(((f32[512,1024]{1,0:T(8,128)}), f32[16,1024]{1,0:T(8,128)}) %reduce-scatter.5.cloned.1.call-update) | async-done | bytes 65552 | tf_op jit(solution)/shard_map/reduce_scatter | solution.py:65
  236.2 0.7 copy.48
  (73 shorter events, 8.7 us)
Async XLA Ops:
  8.0 36.4 %copy-start = (bf16[512,1024]{1,0:T(8,128)(2,1)S(1)}, bf16[512,1024]{1,0:T(8,128)(2,1)}, u32[]{:S(2)}) copy-start(bf16[512,1024]{1,0:T(8,128)(2,1)} %param.17) | copy-start | bytes 3145732
  8.0 1.4 copy-start.9
  8.0 19.1 %copy-start.2 = (f32[512,128]{1,0:T(8,128)S(1)}, f32[512,128]{1,0:T(8,128)}, u32[]{:S(2)}) copy-start(f32[512,128]{1,0:T(8,128)} %param.19) | copy-start | bytes 786436
  8.0 1.3 copy-start.7
  9.3 25.3 %copy-start.10 = (s32[256,2]{0,1:T(2,128)S(1)}, s32[256,2]{0,1:T(2,128)}, u32[]{:S(2)}) copy-start(s32[256,2]{0,1:T(2,128)} %param.13) | copy-start | bytes 6148
  27.1 8.9 %copy-start.17 = (s32[3]{0:T(128)S(1)}, s32[3]{0:T(128)}, u32[]{:S(2)}) copy-start(s32[3]{0:T(128)} %param.24) | copy-start | bytes 40
  31.2 11.6 %all-to-all-start.1 = ((bf16[8,128,128]{2,1,0:T(8,128)(2,1)}), bf16[8,128,128]{2,1,0:T(8,128)(2,1)S(1)}, u32[]{:S(2)}, u32[]{:S(2)}) async-start(bf16[8,128,128]{2,1,0:T(8,128)(2,1)} %bitcast.12), calls=%async_computation.1 | async-start | bytes 524288 | tf_op jit(solution)/shard_map/all_to_all | solution.py:49
  44.4 0.7 copy-start.8
  44.4 0.7 copy-start.13
  44.4 1.2 copy-start.16
  45.1 1.0 copy-start.18
  45.7 0.6 copy-start.14
  46.3 11.9 %copy-start.11 = (s32[3]{0:T(128)S(1)}, s32[3]{0:T(128)}, u32[]{:S(2)}) copy-start(s32[3]{0:T(128)} %compare_select_fusion.5) | copy-start | bytes 40
  47.6 13.0 %copy-start.6 = (f32[1024,128]{1,0:T(8,128)S(1)}, f32[1024,128]{1,0:T(8,128)}, u32[]{:S(2)}) copy-start(f32[1024,128]{1,0:T(8,128)} %param.23) | copy-start | bytes 1572868
  54.1 12.3 %all-to-all-start.2 = ((bf16[8,128,128]{2,1,0:T(8,128)(2,1)}), bf16[8,128,128]{2,1,0:T(8,128)(2,1)}, u32[]{:S(2)}, u32[]{:S(2)}) async-start(bf16[8,128,128]{2,1,0:T(8,128)(2,1)} %bitcast.71), calls=%async_computation.2 | async-start | bytes 524288 | tf_op jit(solution)/shard_map/all_to_all | solution.py:80
  58.1 134.0 %all-reduce.2.cloned.1.call-start = ((), (), s32[]{:S(2)}) async-start(), calls=%async_computation.6 | async-start | bytes 393216 | tf_op jit(solution)/shard_map/psum | solution.py:108
  59.0 14.7 %copy-start.15 = (f32[256]{0:T(256)S(1)}, f32[256]{0:T(256)}, u32[]{:S(2)}) copy-start(f32[256]{0:T(256)} %copy-done.14) | copy-start | bytes 3076
  65.5 129.2 %reduce-scatter.3.cloned.1.call-start = ((), (), s32[]{:S(2)}) async-start(), calls=%async_computation.5 | async-start | bytes 327680 | tf_op jit(solution)/shard_map/reduce_scatter | solution.py:89
  73.4 162.1 %reduce-scatter.5.cloned.1.call-start = ((), (), s32[]{:S(2)}) async-start(), calls=%async_computation.7 | async-start | bytes 2162688 | tf_op jit(solution)/shard_map/reduce_scatter | solution.py:65
  77.0 0.7 copy-start.1
  77.1 4.5 %copy-start.12 = (s32[3]{0:T(128)S(1)}, s32[3]{0:T(128)}, u32[]{:S(2)}) copy-start(s32[3]{0:T(128)} %compare_select_fusion.5) | copy-start | bytes 40
  83.1 153.1 %copy-start.5 = (f32[8,128,128]{2,1,0:T(8,128)}, f32[8,128,128]{2,1,0:T(8,128)S(1)}, u32[]{:S(2)}) copy-start(f32[8,128,128]{2,1,0:T(8,128)S(1)} %scatter_fusion.2) | copy-start | bytes 1572868
  194.0 42.9 %copy-start.4 = (f32[8,128,128]{2,1,0:T(8,128)}, f32[8,128,128]{2,1,0:T(8,128)S(1)}, u32[]{:S(2)}) copy-start(f32[8,128,128]{2,1,0:T(8,128)S(1)} %scatter_fusion.1) | copy-start | bytes 1572868
  194.7 42.2 %copy-start.3 = (f32[8,128,128]{2,1,0:T(8,128)}, f32[8,128,128]{2,1,0:T(8,128)S(1)}, u32[]{:S(2)}) copy-start(f32[8,128,128]{2,1,0:T(8,128)S(1)} %scatter_fusion) | copy-start | bytes 1572868
Sparse Core Ops, SparseCore 0:
  65.7 126.3 all-reduce.1
Sparse Core Ops, SparseCore 1:
  73.5 21.1 reduce-scatter.2
  97.3 138.1 reduce-scatter.4
where the time goes:
time: 245 us; the launch traced here: 244 us
  waiting for transfers between devices  102 us (42%)
  blocking collectives  67 us (27%)
  local copies, waits for them, and re-layouts  30 us (12%)
  other arithmetic  15.8 us (6%)
  between operations  15.8 us (6%)
  starting transfers between devices  7.76 us (3%)
  matrix products  6.01 us (2%)
    psum x1, waiting for transfers between devices, local(): picked_sum, out_grad = lax.psum((picked, head_term), ('dp', 'rep'))  67.7 us
    psum x1, blocking collectives, local(): picked_sum, out_grad = lax.psum((picked, head_term), ('dp', 'rep'))  41 us
    reduce_scatter x1, waiting for transfers between devices, local(): lax.psum_scatter(lax.dot_general(inputs, dhidden, (((0,), (0,)), ((), ())...  27.2 us
    all_to_all x1, blocking collectives, local(): lax.all_to_all(requests, 'dp', split_axis=0, concat_axis=0, tiled=True)  13.6 us
    scatter-add x1, other arithmetic, local(): cold_grad = jnp.zeros((own_rows, width), jnp.float32).at[asked.reshape(-1...  7.07 us
    all_gather x1, blocking collectives, local(): lax.all_gather(accum_updated, 'rep', axis=0, tiled=True)  6.39 us
    all_to_all x1, waiting for transfers between devices, local(): lax.all_to_all(found, 'dp', split_axis=0, concat_axis=0, tiled=True)  6.23 us
    all_gather x1, blocking collectives, local(): lax.all_gather(table_updated, 'rep', axis=0, tiled=True)  6.1 us
  transfers between devices with their start and end apart: 5, of which 4 were waited for; matrix products, arithmetic and copies ran while one was open for 12% of the time, Pallas kernels for 0%

commit v1 on v0

--- a/solution.py
+++ b/solution.py
@@ -105,7 +105,7 @@
     accum_blocks = hot_accum.reshape(blocks_count, BLOCK, width)
     cache_chosen = cache_blocks[refresh_blocks]
     accum_chosen = accum_blocks[refresh_blocks]
-    picked_sum, out_grad = lax.psum((picked, head_term), ("dp", "rep"))
+    picked_sum, out_grad = lax.psum(lax.psum((picked, head_term), "rep"), "dp")
     flush = picked_sum / divisors[:, None, None]
     cache_part, accum_part = adagrad(cache_chosen, accum_chosen, flush)
     hot_cache_new = cache_blocks.at[refresh_blocks].set(cache_part).reshape(hot_count, width)

time: 245 us -> 342 us (1.40)
  waiting for transfers between devices: 102 us -> 216 us
  blocking collectives: 67 us -> 53.5 us
    reduce_scatter x1, waiting for transfers between devices: 27.2 us -> 128 us  [local(): lax.psum_scatter(lax.dot_general(inputs, dhidden, (((0,), (0,)), ((), ())...]
    reduce_scatter x1, waiting for transfers between devices: 0.03 us -> 19.5 us  [local(): lax.psum_scatter(cold_grad, 'rep', scatter_dimension=0, tiled=True)]
    psum x1 -> x2, blocking collectives: 41 us -> 28 us  [local(): picked_sum, out_grad = lax.psum(lax.psum((picked, head_term), 'rep'), 'dp')]
    psum x1 -> x2, waiting for transfers between devices: 67.7 us -> 62.3 us  [local(): picked_sum, out_grad = lax.psum(lax.psum((picked, head_term), 'rep'), 'dp')]
  transfers between devices with their start and end apart: 5 -> 6, of which waited for: 4 -> 5; matrix products, arithmetic and copies ran while one was open for 12% -> 8% of each run, Pallas kernels for 0% -> 0%
where the time goes in v1:
time: 342 us; the launch traced here: 341 us
  waiting for transfers between devices  216 us (63%)
  blocking collectives  53.5 us (16%)
  local copies, waits for them, and re-layouts  28.2 us (8%)
  other arithmetic  15.8 us (5%)
  between operations  14.1 us (4%)
  starting transfers between devices  7.8 us (2%)
  matrix products  6.01 us (2%)
    reduce_scatter x1, waiting for transfers between devices, local(): lax.psum_scatter(lax.dot_general(inputs, dhidden, (((0,), (0,)), ((), ())...  128 us
    psum x2, waiting for transfers between devices, local(): picked_sum, out_grad = lax.psum(lax.psum((picked, head_term), 'rep'), 'dp')  62.3 us
    psum x2, blocking collectives, local(): picked_sum, out_grad = lax.psum(lax.psum((picked, head_term), 'rep'), 'dp')  28 us
    reduce_scatter x1, waiting for transfers between devices, local(): lax.psum_scatter(cold_grad, 'rep', scatter_dimension=0, tiled=True)  19.5 us
    all_to_all x1, blocking collectives, local(): lax.all_to_all(requests, 'dp', split_axis=0, concat_axis=0, tiled=True)  13.6 us
    scatter-add x1, other arithmetic, local(): cold_grad = jnp.zeros((own_rows, width), jnp.float32).at[asked.reshape(-1...  7.08 us
  transfers between devices with their start and end apart: 6, of which 5 were waited for; matrix products, arithmetic and copies ran while one was open for 8% of the time, Pallas kernels for 0%

profile of v1, /device:TPU:0, one launch (start us, length us, event | category | flops | bytes accessed | tf_op | source)
XLA Modules:
  0.0 341.0 jit_solution(10984362844100420754)
XLA Ops:
  7.2 1.2 copy.45
  8.6 1.1 reduce-window.6
  10.1 2.6 scatter_custom_fusion
  12.7 13.6 %all_to_all.22 = s32[8,1,128]{2,1,0:T(1,128)S(1)} all-to-all(s32[8,1,128]{2,1,0:T(1,128)S(1)} %bitcast.82), channel_id=1, replica_groups=mesh['dp'=8,'rep'=4] {'dp'}, dimensions={0} | all-to-all | bytes 8192 | tf_op jit(solution)/shard_map/all_to_all | solution.py:47
  26.3 4.1 %gather_fusion.1 = bf16[1024,128]{1,0:T(8,128)(2,1)} fusion(f32[512,128]{1,0:T(8,128)S(1)} %copy-done.2, s32[1024]{0:T(1024)S(1)} %fusion.17), kind=kCustom, calls=%fused_computation.1 | custom fusion | bytes 528384 | tf_op jit(solution)/shard_map/gather | solution.py:48
  30.4 3.4 %all-to-all-start.1 = ((bf16[8,128,128]{2,1,0:T(8,128)(2,1)}), bf16[8,128,128]{2,1,0:T(8,128)(2,1)S(1)}, u32[]{:S(2)}, u32[]{:S(2)}) async-start(bf16[8,128,128]{2,1,0:T(8,128)(2,1)} %bitcast.12), calls=%async_computation.1 | async-start | bytes 524288 | tf_op jit(solution)/shard_map/all_to_all | solution.py:49
  34.4 1.1 gather_fusion
  36.1 5.9 %all-to-all-done.1 = bf16[8,128,128]{2,1,0:T(8,128)(2,1)S(1)} async-done(((bf16[8,128,128]{2,1,0:T(8,128)(2,1)}), bf16[8,128,128]{2,1,0:T(8,128)(2,1)S(1)}, u32[]{:S(2)}, u32[]{:S(2)}) %all-to-all-start.1) | async-done | bytes 262176 | tf_op jit(solution)/shard_map/all_to_all | solution.py:49
  41.9 1.3 gather_fusion.2
  45.3 1.3 convolution_convert_fusion
  46.6 1.7 reshape.179
  48.3 1.9 fusion.20
  50.2 2.8 scatter_custom_fusion.1
  53.0 4.0 %all-to-all-start.2 = ((bf16[8,128,128]{2,1,0:T(8,128)(2,1)}), bf16[8,128,128]{2,1,0:T(8,128)(2,1)}, u32[]{:S(2)}, u32[]{:S(2)}) async-start(bf16[8,128,128]{2,1,0:T(8,128)(2,1)} %bitcast.71), calls=%async_computation.2 | async-start | bytes 524288 | tf_op jit(solution)/shard_map/all_to_all | solution.py:80
  57.8 3.7 %scatter_custom_fusion.3 = f32[1024,128]{1,0:T(8,128)S(1)} fusion(f32[1024,128]{1,0:T(8,128)S(1)} %copy-done.6, s32[512]{0:T(512)} %bitcast.91, bf16[512,128]{1,0:T(8,128)(2,1)S(1)} %bitcast.72), kind=kCustom, calls=%fused_computation.25 | custom fusion | flops 131072 | bytes 655360 | tf_op jit(solution)/shard_map/scatter-add | solution.py:100
  61.4 1.2 gather_fusion.4
  62.7 33.4 %all-reduce.3.cloned.1.call-done = f32[3,128,128]{2,1,0:T(8,128)} async-done(((f32[3,128,128]{2,1,0:T(8,128)}), f32[3,128,128]{2,1,0:T(8,128)}) %all-reduce.3.cloned.1.call-update) | async-done | bytes 196624 | tf_op jit(solution)/shard_map/psum | solution.py:108
  96.2 7.1 %scatter_custom_fusion.2 = f32[512,128]{1,0:T(8,128)} fusion(s32[1024]{0:T(1024)S(1)} %bitcast.90, bf16[1024,128]{1,0:T(8,128)(2,1)} %bitcast.31, f32[]{:T(128)} %constant.15.clone.1), kind=kCustom, calls=%fused_computation.18 | custom fusion | flops 262144 | bytes 524292 | tf_op jit(solution)/shard_map/scatter-add | solution.py:85
  103.6 3.4 fusion.2
  108.2 1.2 gather_fusion.3
  109.5 1.2 gather_fusion.6
  111.4 1.5 scatter_fusion.2
  113.3 5.7 %psum.30 = f32[1024]{0:T(1024)S(1)} all-reduce(f32[1024]{0:T(1024)S(1)} %bitcast.81), channel_id=1, replica_groups=mesh['dp'=8,'rep'=4] {'rep'}, use_global_device_ids=true, to_apply=%region_14.15 | all-reduce | flops 1024 | bytes 8192 | tf_op jit(solution)/shard_map/psum | solution.py:108
  119.0 22.2 %psum.31 = f32[1024]{0:T(1024)} all-reduce(f32[1024]{0:T(1024)S(1)} %psum.30), channel_id=1, replica_groups=mesh['dp'=8,'rep'=4] {'dp'}, use_global_device_ids=true, to_apply=%region_15.16 | all-reduce | flops 1024 | bytes 8192 | tf_op jit(solution)/shard_map/psum | solution.py:108
  141.2 28.9 %all-reduce.5.cloned.1.call-done = f32[3,128,128]{2,1,0:T(8,128)} async-done(((f32[3,128,128]{2,1,0:T(8,128)}), f32[3,128,128]{2,1,0:T(8,128)}) %all-reduce.5.cloned.1.call-update) | async-done | bytes 196624 | tf_op jit(solution)/shard_map/psum | solution.py:108
  170.2 1.3 multiply_add_fusion
  172.8 19.5 %reduce-scatter.3.cloned.1.call-done = f32[128,128]{1,0:T(8,128)} async-done(((f32[512,128]{1,0:T(8,128)}), f32[128,128]{1,0:T(8,128)}) %reduce-scatter.3.cloned.1.call-update) | async-done | bytes 65552 | tf_op jit(solution)/shard_map/reduce_scatter | solution.py:89
  192.3 0.9 multiply_add_fusion.1
  193.3 5.8 %all_gather.7 = f32[512,128]{1,0:T(8,128)S(1)} all-gather(f32[128,128]{1,0:T(8,128)S(1)} %get-tuple-element.9), channel_id=1, replica_groups=mesh['dp'=8,'rep'=4] {'rep'}, dimensions={0}, use_global_device_ids=true | all-gather | bytes 327680 | tf_op jit(solution)/shard_map/all_gather | solution.py:95
  199.0 6.2 %all_gather.6 = f32[512,128]{1,0:T(8,128)S(1)} all-gather(f32[128,128]{1,0:T(8,128)S(1)} %get-tuple-element.10), channel_id=1, replica_groups=mesh['dp'=8,'rep'=4] {'rep'}, dimensions={0}, use_global_device_ids=true | all-gather | bytes 327680 | tf_op jit(solution)/shard_map/all_gather | solution.py:94
  205.2 127.8 %reduce-scatter.5.cloned.1.call-done = f32[16,1024]{1,0:T(8,128)} async-done(((f32[512,1024]{1,0:T(8,128)}), f32[16,1024]{1,0:T(8,128)}) %reduce-scatter.5.cloned.1.call-update) | async-done | bytes 65552 | tf_op jit(solution)/shard_map/reduce_scatter | solution.py:65
  333.8 0.7 copy.49
  (71 shorter events, 9.0 us)
Async XLA Ops:
  7.2 36.4 %copy-start = (bf16[512,1024]{1,0:T(8,128)(2,1)S(1)}, bf16[512,1024]{1,0:T(8,128)(2,1)}, u32[]{:S(2)}) copy-start(bf16[512,1024]{1,0:T(8,128)(2,1)} %param.17) | copy-start | bytes 3145732
  7.2 1.4 copy-start.9
  7.2 19.1 %copy-start.2 = (f32[512,128]{1,0:T(8,128)S(1)}, f32[512,128]{1,0:T(8,128)}, u32[]{:S(2)}) copy-start(f32[512,128]{1,0:T(8,128)} %param.19) | copy-start | bytes 786436
  7.2 1.3 copy-start.7
  8.5 25.3 %copy-start.10 = (s32[256,2]{0,1:T(2,128)S(1)}, s32[256,2]{0,1:T(2,128)}, u32[]{:S(2)}) copy-start(s32[256,2]{0,1:T(2,128)} %param.13) | copy-start | bytes 6148
  30.4 11.6 %all-to-all-start.1 = ((bf16[8,128,128]{2,1,0:T(8,128)(2,1)}), bf16[8,128,128]{2,1,0:T(8,128)(2,1)S(1)}, u32[]{:S(2)}, u32[]{:S(2)}) async-start(bf16[8,128,128]{2,1,0:T(8,128)(2,1)} %bitcast.12), calls=%async_computation.1 | async-start | bytes 524288 | tf_op jit(solution)/shard_map/all_to_all | solution.py:49
  43.6 0.7 copy-start.8
  43.6 0.7 copy-start.11
  43.6 1.2 copy-start.14
  44.3 1.0 copy-start.15
  44.9 1.7 copy-start.12
  45.3 12.5 %copy-start.6 = (f32[1024,128]{1,0:T(8,128)S(1)}, f32[1024,128]{1,0:T(8,128)}, u32[]{:S(2)}) copy-start(f32[1024,128]{1,0:T(8,128)} %param.23) | copy-start | bytes 1572868
  53.0 43.2 %all-to-all-start.2 = ((bf16[8,128,128]{2,1,0:T(8,128)(2,1)}), bf16[8,128,128]{2,1,0:T(8,128)(2,1)}, u32[]{:S(2)}, u32[]{:S(2)}) async-start(bf16[8,128,128]{2,1,0:T(8,128)(2,1)} %bitcast.71), calls=%async_computation.2 | async-start | bytes 524288 | tf_op jit(solution)/shard_map/all_to_all | solution.py:80
  57.0 39.1 %all-reduce.3.cloned.1.call-start = ((), (), s32[]{:S(2)}) async-start(), calls=%async_computation.6 | async-start | bytes 393216 | tf_op jit(solution)/shard_map/psum | solution.py:108
  62.7 107.5 %all-reduce.5.cloned.1.call-start = ((), (), s32[]{:S(2)}) async-start(), calls=%async_computation.7 | async-start | bytes 393216 | tf_op jit(solution)/shard_map/psum | solution.py:108
  96.2 96.2 %reduce-scatter.3.cloned.1.call-start = ((), (), s32[]{:S(2)}) async-start(), calls=%async_computation.5 | async-start | bytes 327680 | tf_op jit(solution)/shard_map/reduce_scatter | solution.py:89
  103.3 229.7 %reduce-scatter.5.cloned.1.call-start = ((), (), s32[]{:S(2)}) async-start(), calls=%async_computation.8 | async-start | bytes 2162688 | tf_op jit(solution)/shard_map/reduce_scatter | solution.py:65
  106.9 0.7 copy-start.1
  106.9 6.0 %copy-start.13 = (f32[256]{0:T(256)S(1)}, f32[256]{0:T(256)}, u32[]{:S(2)}) copy-start(f32[256]{0:T(256)} %copy-done.12) | copy-start | bytes 3076
  112.9 220.8 %copy-start.5 = (f32[8,128,128]{2,1,0:T(8,128)}, f32[8,128,128]{2,1,0:T(8,128)S(1)}, u32[]{:S(2)}) copy-start(f32[8,128,128]{2,1,0:T(8,128)S(1)} %scatter_fusion.2) | copy-start | bytes 1572868
  172.1 162.4 %copy-start.4 = (f32[8,128,128]{2,1,0:T(8,128)}, f32[8,128,128]{2,1,0:T(8,128)S(1)}, u32[]{:S(2)}) copy-start(f32[8,128,128]{2,1,0:T(8,128)S(1)} %scatter_fusion.1) | copy-start | bytes 1572868
  172.8 161.7 %copy-start.3 = (f32[8,128,128]{2,1,0:T(8,128)}, f32[8,128,128]{2,1,0:T(8,128)S(1)}, u32[]{:S(2)}) copy-start(f32[8,128,128]{2,1,0:T(8,128)S(1)} %scatter_fusion) | copy-start | bytes 1572868
Sparse Core Ops, SparseCore 0:
  62.8 33.2 all-reduce.2
  99.4 70.6 all-reduce.4
  173.2 19.1 reduce-scatter.2
  195.0 137.9 reduce-scatter.4
